TPU v7x, 512 devices: a whole 4x8x8 slice. The times are simulated.
512 devices in a mesh: tile: 64 (over z, x, core), row: 8 (over y).
Axes of the slice: x: 4, y: 8, z: 8, core: 2. Of those that a mesh axis runs over, the one named last changes fastest.
Arguments:
- swath_blocks: bfloat16 [64, 8, 768, 2048], P('tile', 'row'), may hold values from -6 to 6
- footprint: int32 [64, 8, 768, 1], P('tile', 'row'), may hold values from 0 to 511; in each aligned block of 768 rows (0 to 767, 768 to 1535, ..., all dimensions but the last counted through in order) at most 2 rows name the same one
- cell_row: int32 [64, 8, 768], P('tile', 'row'), may hold values from 0 to 127
- tile_pick: int32 [64, 8, 768], P('tile', 'row'), may hold values from 0 to 3
- sensor: int32 [64, 8, 768], P('tile', 'row'), may hold values from 0 to 1
- bandpass_offset: float32 [2, 8, 8], replicated, may hold values from -0.4 to 0.4
- weight_tiles: bfloat16 [4, 256, 256], replicated, may hold values from -0.375 to 0.375
- lookup_table: float32 [8, 33], replicated, may hold values from 0.5 to 2
- lookup_bin: int32 [64, 1024, 256], P('tile', 'row'), may hold values from 0 to 31
- lookup_frac: float32 [64, 1024, 256], P('tile', 'row'), may hold values from 0 to 1
- brdf_params: float32 [8, 3], replicated, may hold values from 0.05 to 1
- vol_kernel: float32 [64, 1024, 256], P('tile', 'row'), may hold values from 0.1 to 2
- geo_kernel: float32 [64, 1024, 256], P('tile', 'row'), may hold values from 0.1 to 2
- clear_mask: int32 [64, 1024, 256], P('tile', 'row'), may hold values 0 or 1
Outputs:
- nbar: bfloat16 [64, 1024, 2048], P('tile', 'row')
Inputs may be any that keep to these rules, and one draw needn't show every extreme that they name: `footprint`: at most 2 of the blocks of one device name one destination, and in every draw some destination is named by exactly 2 of them.
All inputs are finite; a program needn't handle non-finite values. No bound on the sum of `clear_mask` on one device may be relied on, other than what follows from the above.
Results may differ from a plain program's by a relative error of at most 0.0057.
Values may be sent and summed in bfloat16 or wider, within the bound.
A program may use at most 64 MiB of HBM per device.

v0:
```python
import jax
import jax.numpy as jnp
from jax import lax
from jax.sharding import PartitionSpec as P

nadir_volume = 0.3
nadir_geometric = 0.6


def with_halo(block, sides, width):
    for axis, dim in sides:
        count = lax.axis_size(axis)
        forward = [(i, i + 1) for i in range(count - 1)]
        backward = [(target, source) for source, target in forward]
        low = lax.ppermute(
            lax.slice_in_dim(block, block.shape[dim] - width, None, axis=dim), axis, forward
        )
        high = lax.ppermute(lax.slice_in_dim(block, 0, width, axis=dim), axis, backward)
        block = jnp.concatenate([low, block, high], axis=dim)
    return block


def resample_rows(rows_in, tag_codes, mixing, stacked_weights, band_count, tile_count):
    slot_count = rows_in.shape[0]
    row_width = rows_in.shape[1]
    pixels = row_width // band_count
    group_size = slot_count // 8

    def resample_group(operands):
        payload, codes_here = operands
        sensor_g = codes_here % 2
        tile_g = codes_here // 2 % tile_count
        chosen_mix = jnp.where(sensor_g[:, None, None] == 1, mixing[1][None], mixing[0][None])
        banded = jnp.einsum(
            "ons,osi->oni",
            chosen_mix,
            payload.reshape(group_size, band_count, pixels).astype(jnp.float32),
            precision=lax.Precision.HIGHEST,
        ).astype(jnp.bfloat16)
        chosen = tile_g[:, None] == jnp.arange(tile_count, dtype=jnp.int32)[None, :]
        spread = jnp.where(
            chosen[:, None, :, None], banded[:, :, None, :], jnp.zeros((), jnp.bfloat16)
        )
        result = jnp.dot(
            spread.reshape(group_size * band_count, tile_count * pixels),
            stacked_weights,
            preferred_element_type=jnp.float32,
        )
        return result.astype(jnp.bfloat16).reshape(group_size, row_width)

    grouped = lax.map(
        resample_group,
        (rows_in.reshape(8, group_size, row_width), tag_codes.reshape(8, group_size)),
    )
    return grouped.reshape(slot_count, row_width)


def on_device(
    swath_blocks,
    footprint,
    cell_row,
    tile_pick,
    sensor,
    bandpass_offset,
    weight_tiles,
    lookup_table,
    lookup_bin,
    lookup_frac,
    brdf_params,
    vol_kernel,
    geo_kernel,
    clear_mask,
):
    tile_devices = lax.axis_size("tile")
    row_devices = lax.axis_size("row")
    destinations = tile_devices * row_devices
    block_count = swath_blocks.shape[2]
    row_width = swath_blocks.shape[3]
    band_count = bandpass_offset.shape[1]
    pixels = row_width // band_count
    tile_count = weight_tiles.shape[0]
    grid_rows = lookup_bin.shape[1]
    bin_count = lookup_table.shape[1] - 1
    capacity = max(2, 3 * block_count // (2 * destinations))
    mixing = jnp.eye(band_count, dtype=jnp.float32)[None, :, :] + bandpass_offset
    stacked_weights = weight_tiles.reshape(tile_count * pixels, pixels)
    blocks = swath_blocks.reshape(block_count, row_width)
    target = footprint.reshape(block_count)
    tag_codes = (
        cell_row.reshape(block_count) * tile_count + tile_pick.reshape(block_count)
    ) * 2 + sensor.reshape(block_count)
    order_index = jnp.arange(block_count, dtype=jnp.int32)
    same_dest = target[:, None] == target[None, :]
    earlier = order_index[:, None] > order_index[None, :]
    slot_rank = jnp.sum(jnp.logical_and(same_dest, earlier).astype(jnp.int32), axis=1)
    position = target * capacity + slot_rank
    buffer = jnp.zeros((destinations * capacity, row_width), jnp.bfloat16).at[position].set(blocks)
    buffer = buffer.reshape(tile_devices, row_devices, capacity, row_width)
    tag_buffer = jnp.full((destinations * capacity,), -1, jnp.int32).at[position].set(tag_codes)
    tag_buffer = tag_buffer.reshape(tile_devices, row_devices, capacity)
    received, arrived_tags = (
        lax.all_to_all(
            lax.all_to_all(buffer, "tile", split_axis=0, concat_axis=0, tiled=True),
            "row",
            split_axis=1,
            concat_axis=1,
            tiled=True,
        ),
        lax.all_to_all(
            lax.all_to_all(tag_buffer, "tile", split_axis=0, concat_axis=0, tiled=True),
            "row",
            split_axis=1,
            concat_axis=1,
            tiled=True,
        ),
    )
    received_rows = received.reshape(destinations * capacity, row_width)
    clipped = jnp.maximum(arrived_tags.reshape(destinations * capacity), 0)
    arrived_rows = resample_rows(
        received_rows, clipped, mixing, stacked_weights, band_count, tile_count
    )
    target_row = clipped // (2 * tile_count)
    accum_grid = (
        jnp.zeros((grid_rows, row_width), jnp.float32)
        .at[target_row]
        .add(arrived_rows.astype(jnp.float32))
    )
    padded = with_halo(accum_grid, (("row", 0),), 1)
    smoothed = 0.25 * padded[:-2] + 0.5 * padded[1:-1] + 0.25 * padded[2:]
    smoothed = smoothed.reshape(grid_rows, band_count, pixels)
    bin_index = lookup_bin[0]
    fraction = lookup_frac[0][:, None, :]
    onehot = (
        bin_index[:, :, None] == jnp.arange(bin_count, dtype=jnp.int32)[None, None, :]
    ).astype(jnp.float32)
    lower_value = jnp.einsum(
        "rpn,bn->rbp", onehot, lookup_table[:, :-1], precision=lax.Precision.HIGHEST
    )
    upper_value = jnp.einsum(
        "rpn,bn->rbp", onehot, lookup_table[:, 1:], precision=lax.Precision.HIGHEST
    )
    table_value = lower_value * (1.0 - fraction) + upper_value * fraction
    isotropic = brdf_params[:, 0][None, :, None]
    volume = brdf_params[:, 1][None, :, None]
    geometric = brdf_params[:, 2][None, :, None]
    numerator = isotropic + volume * nadir_volume + geometric * nadir_geometric
    denominator = (
        isotropic + volume * vol_kernel[0][:, None, :] + geometric * geo_kernel[0][:, None, :]
    )
    cfactor = numerator / denominator
    result = smoothed * table_value * cfactor * clear_mask[0][:, None, :].astype(jnp.float32)
    return result.reshape(1, grid_rows, row_width).astype(jnp.bfloat16)


def solution(mesh):
    in_specs = (
        P("tile", "row", None, None),
        P("tile", "row", None, None),
        P("tile", "row", None),
        P("tile", "row", None),
        P("tile", "row", None),
        P(),
        P(),
        P(),
        P("tile", "row", None),
        P("tile", "row", None),
        P(),
        P("tile", "row", None),
        P("tile", "row", None),
        P("tile", "row", None),
    )
    out_specs = P("tile", "row", None)
    return jax.shard_map(
        on_device, mesh=mesh, in_specs=in_specs, out_specs=out_specs, check_vma=False
    )
```

profile of v0, /device:TPU:70, one launch (start us, length us, event | category | flops | bytes accessed | tf_op | source)
XLA Modules:
  0.0 383.5 jit_solution(9151351784373132201)
XLA Ops:
  2.7 3.4 scatter_custom_fusion
  7.3 12.9 %all-to-all-start = ((s32[64,8,2]{1,2,0:T(2,128)}), s32[64,8,2]{1,2,0:T(2,128)S(1)}, u32[]{:S(2)}, u32[]{:S(2)}) async-start(s32[64,8,2]{1,2,0:T(2,128)} %copy.34), calls=%async_computation | async-start | bytes 131072 | tf_op jit(solution)/shard_map/all_to_all | solution.py:110
  20.2 9.4 %scatter_custom_fusion.1 = bf16[1024,2048]{1,0:T(8,128)(2,1)} fusion(s32[768]{0:T(1024)S(1)} %fusion.36, bf16[1,1,768,2048]{3,2,1,0:T(8,128)(2,1)S(1)} %copy-done, bf16[]{:T(256)} %constant.118.clone.1), kind=kCustom, calls=%fused_computation.32 | custom fusion | bytes 7340034 | tf_op jit(solution)/shard_map/scatter | solution.py:97
  29.6 7.7 %reshape.291 = bf16[64,8,2,2048]{3,2,1,0:T(2,128)(2,1)} reshape(bf16[1024,2048]{1,0:T(8,128)(2,1)} %scatter_custom_fusion.1) | data formatting | bytes 8388608 | tf_op jit(solution)/shard_map/reshape | solution.py:98
  37.3 10.5 %all-to-all-start.2 = ((bf16[64,8,2,2048]{3,2,1,0:T(2,128)(2,1)}), bf16[64,8,2,2048]{3,2,1,0:T(2,128)(2,1)}, u32[]{:S(2)}, u32[]{:S(2)}) async-start(bf16[64,8,2,2048]{3,2,1,0:T(2,128)(2,1)} %reshape.291), calls=%async_computation.2 | async-start | bytes 8388608 | tf_op jit(solution)/shard_map/all_to_all | solution.py:103
  48.5 94.5 %all-to-all-done.2 = bf16[64,8,2,2048]{3,2,1,0:T(2,128)(2,1)} async-done(((bf16[64,8,2,2048]{3,2,1,0:T(2,128)(2,1)}), bf16[64,8,2,2048]{3,2,1,0:T(2,128)(2,1)}, u32[]{:S(2)}, u32[]{:S(2)}) %all-to-all-start.2) | async-done | bytes 4194336 | tf_op jit(solution)/shard_map/all_to_all | solution.py:103
  143.1 7.1 %all-to-all-start.1 = ((s32[8,1,128]{2,1,0:T(1,128)}), s32[8,1,128]{2,1,0:T(1,128)S(1)}, u32[]{:S(2)}, u32[]{:S(2)}) async-start(s32[8,1,128]{2,1,0:T(1,128)} %reshape.330), calls=%async_computation.1 | async-start | bytes 8192 | tf_op jit(solution)/shard_map/all_to_all | solution.py:109
  150.2 7.6 %copy.40 = bf16[64,8,2,2048]{3,2,0,1:T(2,128)(2,1)} copy(bf16[64,8,2,2048]{3,2,1,0:T(2,128)(2,1)} %all-to-all-done.2) | data formatting | bytes 8388608 | tf_op jit(solution)/shard_map/all_to_all | solution.py:103
  157.8 7.3 %all-to-all-start.3 = ((bf16[64,8,2,2048]{3,2,0,1:T(2,128)(2,1)}), bf16[64,8,2,2048]{3,2,0,1:T(2,128)(2,1)}, u32[]{:S(2)}, u32[]{:S(2)}) async-start(bf16[64,8,2,2048]{3,2,0,1:T(2,128)(2,1)} %copy.40), calls=%async_computation.3 | async-start | bytes 8388608 | tf_op jit(solution)/shard_map/all_to_all | solution.py:102
  167.8 2.4 fusion.20
  176.4 84.8 %all-to-all-done.3 = bf16[64,8,2,2048]{3,2,0,1:T(2,128)(2,1)} async-done(((bf16[64,8,2,2048]{3,2,0,1:T(2,128)(2,1)}), bf16[64,8,2,2048]{3,2,0,1:T(2,128)(2,1)}, u32[]{:S(2)}, u32[]{:S(2)}) %all-to-all-start.3) | async-done | bytes 4194336 | tf_op jit(solution)/shard_map/all_to_all | solution.py:102
  261.2 9.1 %copy.41 = bf16[64,8,2,2048]{3,2,1,0:T(2,128)(2,1)} copy(bf16[64,8,2,2048]{3,2,0,1:T(2,128)(2,1)} %all-to-all-done.3) | data formatting | bytes 8388608 | tf_op jit(solution)/shard_map/all_to_all | solution.py:102
  270.3 7.3 %reshape_reshape.3 = bf16[8,128,2048]{2,1,0:T(8,128)(2,1)} reshape(bf16[64,8,2,2048]{3,2,1,0:T(2,128)(2,1)} %copy.41) | data formatting | bytes 8388608 | tf_op jit(solution)/shard_map/reshape;reshape | solution.py:53
  277.5 74.1 %while.13 = (s32[]{:T(128)}, bf16[8,128,2048]{2,1,0:T(8,128)(2,1)}, s32[8,128]{1,0:T(8,128)S(1)}, f32[2,8,8]{2,1,0:T(8,128)S(1)}, bf16[8,128,2048]{2,1,0:T(8,128)(2,1)}, /*index=5*/bf16[1024,256]{1,0:T(8,128)(2,1)}, s32[]{:T(128)}) while((s32[]{:T(128)}, bf16[8,128,2048]{2,1,0:T(8,128)(2,1)}, s32[8,128]{1,0:T(8,128)S(1)}, ...), condition=%wide.region_4.5_spmd, body=%wide.region_3.4_spmd.sunk | while | flops 563622784 | bytes 17308020 | solution.py:51
  282.8 2.1 broadcast_in_dim.140
  292.1 2.1 broadcast_in_dim.140
  301.3 2.1 broadcast_in_dim.140
  303.4 1.9 constant_dynamic-update-slice_fusion.2
  310.6 2.1 broadcast_in_dim.140
  319.8 2.1 broadcast_in_dim.140
  329.1 2.1 broadcast_in_dim.140
  331.2 1.9 constant_dynamic-update-slice_fusion.2
  338.3 2.1 broadcast_in_dim.140
  340.4 1.9 constant_dynamic-update-slice_fusion.2
  347.6 2.1 broadcast_in_dim.140
  349.7 1.9 constant_dynamic-update-slice_fusion.2
  351.6 15.8 %scatter_custom_fusion.2 = f32[128,2048]{1,0:T(8,128)} fusion(s32[1024]{0:T(1024)} %bitcast.101, bf16[1024,2048]{1,0:T(8,128)(2,1)} %bitcast.92, f32[]{:T(128)} %constant.108.clone.1), kind=kCustom, calls=%fused_computation.27 | custom fusion | flops 4194304 | bytes 5243392 | tf_op jit(solution)/shard_map/scatter-add | solution.py:126
  368.5 2.2 collective-permute-start
  372.0 4.2 %collective-permute-done.1 = f32[1,2048]{1,0:T(1,128)S(1)} collective-permute-done((f32[1,2048]{1,0:T(1,128)S(1)}, f32[1,2048]{1,0:T(1,128)S(1)}, u32[]{:S(2)}, u32[]{:S(2)}) %collective-permute-start.1) | collective-permute-done | bytes 8224 | tf_op jit(solution)/shard_map/ppermute | solution.py:18
  376.2 2.3 fusion.26
  378.9 2.5 fusion.24
  381.4 2.1 convert_element_type.64
  (165 shorter events, 65.3 us)
Async XLA Ops:
  0.0 20.2 %copy-start = (bf16[1,1,768,2048]{3,2,1,0:T(8,128)(2,1)S(1)}, bf16[1,1,768,2048]{3,2,1,0:T(8,128)(2,1)}, u32[]{:S(2)}) copy-start(bf16[1,1,768,2048]{3,2,1,0:T(8,128)(2,1)} %param.16) | copy-start | bytes 9437188
  7.3 30.0 %all-to-all-start = ((s32[64,8,2]{1,2,0:T(2,128)}), s32[64,8,2]{1,2,0:T(2,128)S(1)}, u32[]{:S(2)}, u32[]{:S(2)}) async-start(s32[64,8,2]{1,2,0:T(2,128)} %copy.34), calls=%async_computation | async-start | bytes 131072 | tf_op jit(solution)/shard_map/all_to_all | solution.py:110
  37.3 105.8 %all-to-all-start.2 = ((bf16[64,8,2,2048]{3,2,1,0:T(2,128)(2,1)}), bf16[64,8,2,2048]{3,2,1,0:T(2,128)(2,1)}, u32[]{:S(2)}, u32[]{:S(2)}) async-start(bf16[64,8,2,2048]{3,2,1,0:T(2,128)(2,1)} %reshape.291), calls=%async_computation.2 | async-start | bytes 8388608 | tf_op jit(solution)/shard_map/all_to_all | solution.py:103
  143.1 14.8 %all-to-all-start.1 = ((s32[8,1,128]{2,1,0:T(1,128)}), s32[8,1,128]{2,1,0:T(1,128)S(1)}, u32[]{:S(2)}, u32[]{:S(2)}) async-start(s32[8,1,128]{2,1,0:T(1,128)} %reshape.330), calls=%async_computation.1 | async-start | bytes 8192 | tf_op jit(solution)/shard_map/all_to_all | solution.py:109
  157.8 7.4 %copy-start.7 = (f32[8,3]{0,1:T(4,128)S(1)}, f32[8,3]{0,1:T(4,128)}, u32[]{:S(2)}) copy-start(f32[8,3]{0,1:T(4,128)} %param.26) | copy-start | bytes 292
  157.8 8.7 %copy-start.2 = (f32[1,128,256]{2,1,0:T(8,128)S(1)}, f32[1,128,256]{2,1,0:T(8,128)}, u32[]{:S(2)}) copy-start(f32[1,128,256]{2,1,0:T(8,128)} %param.25) | copy-start | bytes 393220
  157.8 9.3 %copy-start.4 = (s32[1,128,256]{2,1,0:T(8,128)S(1)}, s32[1,128,256]{2,1,0:T(8,128)}, u32[]{:S(2)}) copy-start(s32[1,128,256]{2,1,0:T(8,128)} %param.29) | copy-start | bytes 393220
  157.8 10.0 %copy-start.3 = (s32[1,128,256]{2,1,0:T(8,128)S(1)}, s32[1,128,256]{2,1,0:T(8,128)}, u32[]{:S(2)}) copy-start(s32[1,128,256]{2,1,0:T(8,128)} %param.24) | copy-start | bytes 393220
  157.8 10.0 %copy-start.9 = (f32[8,33]{1,0:T(8,128)S(1)}, f32[8,33]{1,0:T(8,128)}, u32[]{:S(2)}) copy-start(f32[8,33]{1,0:T(8,128)} %param.23) | copy-start | bytes 3172
  157.8 103.4 %all-to-all-start.3 = ((bf16[64,8,2,2048]{3,2,0,1:T(2,128)(2,1)}), bf16[64,8,2,2048]{3,2,0,1:T(2,128)(2,1)}, u32[]{:S(2)}, u32[]{:S(2)}) async-start(bf16[64,8,2,2048]{3,2,0,1:T(2,128)(2,1)} %copy.40), calls=%async_computation.3 | async-start | bytes 8388608 | tf_op jit(solution)/shard_map/all_to_all | solution.py:102
  278.8 2.5 copy-start.14
  288.0 2.5 copy-start.14
  297.2 2.5 copy-start.14
  306.5 2.5 copy-start.14
  315.8 2.5 copy-start.14
  325.0 2.5 copy-start.14
  334.3 2.5 copy-start.14
  343.6 2.5 copy-start.14
  351.6 20.3 %copy-start.8 = (f32[8,3]{0,1:T(4,128)S(1)}, f32[8,3]{0,1:T(4,128)}, u32[]{:S(2)}) copy-start(f32[8,3]{0,1:T(4,128)} %param.26) | copy-start | bytes 292
  351.6 27.2 %copy-start.5 = (f32[128,256]{1,0:T(8,128)S(1)}, f32[128,256]{1,0:T(8,128)}, u32[]{:S(2)}) copy-start(f32[128,256]{1,0:T(8,128)} %broadcast_subtract_fusion) | copy-start | bytes 393220
  351.6 27.2 %copy-start.6 = (f32[128,256]{1,0:T(8,128)S(1)}, f32[128,256]{1,0:T(8,128)}, u32[]{:S(2)}) copy-start(f32[128,256]{1,0:T(8,128)} %convert_bitcast_fusion) | copy-start | bytes 393220
  351.6 27.3 %copy-start.10 = (f32[8,33]{1,0:T(8,128)S(1)}, f32[8,33]{1,0:T(8,128)}, u32[]{:S(2)}) copy-start(f32[8,33]{1,0:T(8,128)} %param.23) | copy-start | bytes 3172
  367.4 11.4 %copy-start.1 = (f32[128,256,8]{1,2,0:T(8,128)S(1)}, f32[128,256,8]{1,2,0:T(8,128)}, u32[]{:S(2)}) copy-start(f32[128,256,8]{1,2,0:T(8,128)} %fusion.20) | copy-start | bytes 3145732
  367.5 11.4 %copy-start.11 = (f32[8]{0:T(128)S(1)}, f32[8]{0:T(128)}, u32[]{:S(2)}) copy-start(f32[8]{0:T(128)} %get-tuple-element.133) | copy-start | bytes 100
  367.5 11.4 %copy-start.12 = (f32[8]{0:T(128)S(1)}, f32[8]{0:T(128)}, u32[]{:S(2)}) copy-start(f32[8]{0:T(128)} %get-tuple-element.134) | copy-start | bytes 100
  367.5 11.4 %copy-start.13 = (f32[8]{0:T(128)S(1)}, f32[8]{0:T(128)}, u32[]{:S(2)}) copy-start(f32[8]{0:T(128)} %get-tuple-element.135) | copy-start | bytes 100
  367.5 11.5 %copy-start.15 = (f32[1,128,256]{2,1,0:T(8,128)S(1)}, f32[1,128,256]{2,1,0:T(8,128)}, u32[]{:S(2)}) copy-start(f32[1,128,256]{2,1,0:T(8,128)} %param.28) | copy-start | bytes 393220
  367.5 11.5 %copy-start.16 = (f32[1,128,256]{2,1,0:T(8,128)S(1)}, f32[1,128,256]{2,1,0:T(8,128)}, u32[]{:S(2)}) copy-start(f32[1,128,256]{2,1,0:T(8,128)} %param.27) | copy-start | bytes 393220
  368.5 3.5 collective-permute-start
  370.6 5.5 %collective-permute-start.1 = (f32[1,2048]{1,0:T(1,128)S(1)}, f32[1,2048]{1,0:T(1,128)S(1)}, u32[]{:S(2)}, u32[]{:S(2)}) collective-permute-start(f32[1,2048]{1,0:T(1,128)S(1)} %get-tuple-element.130), channel_id=1, source_target_pairs={{1,0},{2,1},{3,2},{4,3},{5,4},{6,5},{7,6},{9,8},{10,9},{11,10},{12... | collective-permute-start | bytes 24584 | tf_op jit(solution)/shard_map/ppermute | solution.py:18
where the time goes:
time: 386 us; the launch traced here: 383 us
  waiting for transfers between devices  184 us (48%)
  local copies, waits for them, and re-layouts  99.6 us (26%)
  starting transfers between devices  41.3 us (11%)
  other arithmetic  36.3 us (9%)
  matrix products  22 us (6%)
    all_to_all x1, waiting for transfers between devices, on_device(): lax.all_to_all(buffer, 'tile', split_axis=0, concat_axis=0, tiled=True)  94.5 us
    all_to_all x1, waiting for transfers between devices, on_device(): lax.all_to_all(lax.all_to_all(buffer, 'tile', split_axis=0, concat_axis=0...  84.8 us
    broadcast_in_dim x8, local copies, waits for them, and re-layouts, resample_rows(): lax.map(resample_group, (rows_in.reshape(8, group_size, row_width), tag_c...  16.8 us
    scatter-add x1, other arithmetic, on_device(): accum_grid = jnp.zeros((grid_rows, row_width), jnp.float32).at[target_row...  15.8 us
    dynamic_update_slice x8, local copies, waits for them, and re-layouts, resample_rows(): lax.map(resample_group, (rows_in.reshape(8, group_size, row_width), tag_c...  15.1 us
    all_to_all x1, starting transfers between devices, on_device(): lax.all_to_all(tag_buffer, 'tile', split_axis=0, concat_axis=0, tiled=True)  12.9 us
    dot_general x8, matrix products, resample_group(): jnp.dot(spread.reshape(group_size * band_count, tile_count * pixels), sta...  12 us
    all_to_all x1, starting transfers between devices, on_device(): lax.all_to_all(buffer, 'tile', split_axis=0, concat_axis=0, tiled=True)  10.5 us
  transfers between devices with their start and end apart: 6, of which 3 were waited for; matrix products, arithmetic and copies ran while one was open for 10% of the time, Pallas kernels for 0%

commit v1 on v0

v1 whole, which is shorter than its diff:
```python
import functools

import jax
import jax.numpy as jnp
from jax import lax
from jax.experimental import pallas as pl
from jax.experimental.pallas import tpu as pltpu
from jax.sharding import PartitionSpec as P

nadir_volume = 0.3
nadir_geometric = 0.6
MESH = pl.DeviceIdType.MESH
CHUNKS = 4
HALF = 128


def offsets(t):
    spread = (t // 64 + t) % 8
    return t % 8, (t // 8 + t) % 8, spread // 2, spread % 2


def slot_of(target, rank, group):
    tile = lax.axis_index("tile")
    row = lax.axis_index("row")
    to_tile, to_row = target // 8, target % 8
    dy = (to_row - row) % 8
    dz = (to_tile // 8 - tile // 8) % 8
    dx = ((to_tile // 2) % 4 - (tile // 2) % 4) % 4
    dc = (to_tile % 2 - tile % 2) % 2
    t = ((dx * 2 + dc - dy) % 8) * 64 + ((dz - dy) % 8) * 8 + dy
    return ((t // group) * 2 + rank) * group + t % group


def kernel(
    mixing_ref,
    table_ref,
    brdf_ref,
    blocks_ref,
    position_ref,
    code_ref,
    weights_ref,
    bin_ref,
    frac_ref,
    vol_ref,
    geo_ref,
    mask_ref,
    out_ref,
    outgoing,
    incoming,
    tags_out,
    tags_in,
    unpacked,
    sums,
    resampled,
    grid,
    factor,
    edge_out,
    edge_in,
    send_sem,
    recv_sem,
    tag_send_sem,
    tag_recv_sem,
    edge_send_sem,
    edge_recv_sem,
):
    devices = outgoing.shape[0]
    blocks = blocks_ref.shape[0]
    bands = 8
    pixels = 256
    cells = out_ref.shape[0]
    group = devices // CHUNKS
    tile = lax.axis_index("tile")
    row = lax.axis_index("row")
    z, x, core = tile // 8, (tile // 2) % 4, tile % 2

    lane = lax.broadcasted_iota(jnp.int32, (group, 128), 1)
    for k in range(CHUNKS):
        slot_number = lax.broadcasted_iota(jnp.int32, (2 * group, blocks), 0) + k * 2 * group
        holds = position_ref[...] == slot_number
        code = jnp.sum(jnp.where(holds, code_ref[...] + 1, 0), axis=1, keepdims=True) - 1
        tags_out[pl.ds(k * group, group)] = jnp.where(
            lane == 0, code[:group], code[group:]
        ).reshape(group, 1, 128)
        chosen = holds.astype(jnp.bfloat16)
        for b in range(bands):
            moved = jnp.dot(
                chosen, blocks_ref[:, pl.ds(b * pixels, pixels)], preferred_element_type=jnp.float32
            )
            for slot in range(2):
                for h in range(pixels // HALF):
                    unpacked[
                        pl.ds((h * group * 2 + slot) * bands + b, group, stride=2 * bands), :
                    ] = moved[slot * group : (slot + 1) * group, h * HALF : (h + 1) * HALF]
        for i in range(group // 32):
            halves = [
                unpacked[pl.ds((h * group + i * 32) * 2 * bands, 512), :]
                for h in range(pixels // HALF)
            ]
            outgoing[pl.ds(k * group + i * 32, 32)] = (
                jnp.concatenate(halves, axis=1).astype(jnp.bfloat16).reshape(32, 2 * bands, pixels)
            )
        if k == 0:
            incoming[0] = outgoing[0]
            tags_in[0] = tags_out[0]

        @pl.loop(max(1, k * group), (k + 1) * group)
        def _(t):
            dy, dz, dx, dc = offsets(t)
            to_tile = ((z + dz) % 8) * 8 + ((x + dx) % 4) * 2 + (core + dc) % 2
            to_row = (row + dy) % 8
            pltpu.make_async_remote_copy(
                src_ref=outgoing.at[t],
                dst_ref=incoming.at[t],
                send_sem=send_sem,
                recv_sem=recv_sem.at[k],
                device_id=(to_tile, to_row),
                device_id_type=MESH,
            ).start()
            pltpu.make_async_remote_copy(
                src_ref=tags_out.at[t],
                dst_ref=tags_in.at[t],
                send_sem=tag_send_sem,
                recv_sem=tag_recv_sem.at[k],
                device_id=(to_tile, to_row),
                device_id_type=MESH,
            ).start()

    bins = table_ref.shape[1] - 1

    @pl.loop(0, cells // 8)
    def _(g):
        rows = pl.ds(pl.multiple_of(g * 8, 8), 8)
        which = bin_ref[rows, :]
        part = frac_ref[rows, :]
        volume_angle = vol_ref[rows, :]
        geometric_angle = geo_ref[rows, :]
        keep = mask_ref[rows, :].astype(jnp.float32)
        lower = [jnp.full((8, pixels), table_ref[b, 0]) for b in range(bands)]
        upper = [jnp.full((8, pixels), table_ref[b, 1]) for b in range(bands)]
        for n in range(1, bins):
            here = which == n
            for b in range(bands):
                lower[b] = jnp.where(here, table_ref[b, n], lower[b])
                upper[b] = jnp.where(here, table_ref[b, n + 1], upper[b])
        for b in range(bands):
            value = lower[b] * (1.0 - part) + upper[b] * part
            isotropic, volume, geometric = brdf_ref[b, 0], brdf_ref[b, 1], brdf_ref[b, 2]
            numerator = isotropic + volume * nadir_volume + geometric * nadir_geometric
            denominator = isotropic + volume * volume_angle + geometric * geometric_angle
            factor[rows, pl.ds(b * pixels, pixels)] = value * (numerator / denominator) * keep

    codes = sums.shape[0]
    for k in range(CHUNKS):
        low = max(1, k * group)
        part = pl.ds(low, (k + 1) * group - low)
        pltpu.make_async_copy(tags_in.at[part], tags_in.at[part], tag_recv_sem.at[k]).wait()
        pltpu.make_async_copy(incoming.at[part], incoming.at[part], recv_sem.at[k]).wait()
        for i in range(group // 32):
            arrived = incoming[pl.ds(k * group + i * 32, 32)]
            for h in range(pixels // HALF):
                unpacked[pl.ds((h * group + i * 32) * 2 * bands, 512), :] = (
                    arrived[:, :, h * HALF : (h + 1) * HALF].reshape(512, HALF).astype(jnp.float32)
                )
        tag_rows = jnp.transpose(tags_in[pl.ds(k * group, group)].reshape(group, 128))
        code = lax.broadcasted_iota(jnp.int32, (codes, group), 0)
        chosen = jnp.concatenate(
            [(tag_rows[slot : slot + 1, :] == code).astype(jnp.bfloat16) for slot in range(2)],
            axis=1,
        )
        for b in range(bands):
            for h in range(pixels // HALF):
                values = jnp.concatenate(
                    [
                        unpacked[
                            pl.ds(
                                h * group * 2 * bands + slot * bands + b, group, stride=2 * bands
                            ),
                            :,
                        ]
                        for slot in range(2)
                    ],
                    axis=0,
                ).astype(jnp.bfloat16)
                lanes = pl.ds(b * pixels + h * HALF, HALF)
                added = jnp.dot(chosen, values, preferred_element_type=jnp.float32)
                if k == 0:
                    sums[:, lanes] = added
                else:
                    sums[:, lanes] += added

    picks = weights_ref.shape[0]
    for b in range(bands):
        lanes = pl.ds(b * pixels, pixels)
        total = None
        for pick in range(picks):
            rows = pl.ds(pick * 2 * cells, 2 * cells)
            term = jnp.dot(
                sums[rows, lanes].astype(jnp.bfloat16),
                weights_ref[pick],
                preferred_element_type=jnp.float32,
            )
            total = term if total is None else total + term
        resampled[:, lanes] = total

    @pl.loop(0, cells // 8)
    def _(g):
        start = pl.multiple_of(g * 8, 8)
        for b in range(bands):
            total = None
            for s in range(2):
                for other in range(bands):
                    term = (
                        mixing_ref[s, b * bands + other]
                        * resampled[
                            pl.ds(pl.multiple_of(s * cells + start, 8), 8),
                            pl.ds(other * pixels, pixels),
                        ]
                    )
                    total = term if total is None else total + term
            grid[pl.ds(pl.multiple_of(start + 8, 8), 8), pl.ds(b * pixels, pixels)] = total

    edge_out[0] = grid[pl.ds(8 + cells - 1, 1), :]
    edge_out[1] = grid[pl.ds(8, 1), :]
    copies = [
        pltpu.make_async_remote_copy(
            src_ref=edge_out.at[side],
            dst_ref=edge_in.at[side],
            send_sem=edge_send_sem.at[side],
            recv_sem=edge_recv_sem.at[side],
            device_id=(tile, (row + step) % 8),
            device_id_type=MESH,
        )
        for side, step in ((0, 1), (1, 7))
    ]
    for copy in copies:
        copy.start()
    for copy in copies:
        copy.wait()
    grid[pl.ds(7, 1), :] = jnp.where(row == 0, 0.0, edge_in[0])
    grid[pl.ds(8 + cells, 1), :] = jnp.where(row == 7, 0.0, edge_in[1])
    for g in range(cells // 16):
        above = grid[pl.ds(g * 16 + 7, 16), :]
        here = grid[pl.ds(g * 16 + 8, 16), :]
        below = grid[pl.ds(g * 16 + 9, 16), :]
        smoothed = 0.25 * above + 0.5 * here + 0.25 * below
        rows = pl.ds(g * 16, 16)
        out_ref[rows, :] = (smoothed * factor[rows, :]).astype(jnp.bfloat16)

    rest = pl.ds(1, devices - 1)
    pltpu.make_async_copy(outgoing.at[rest], outgoing.at[rest], send_sem).wait()
    pltpu.make_async_copy(tags_in.at[rest], tags_in.at[rest], tag_send_sem).wait()


def on_device(
    swath_blocks,
    footprint,
    cell_row,
    tile_pick,
    sensor,
    bandpass_offset,
    weight_tiles,
    lookup_table,
    lookup_bin,
    lookup_frac,
    brdf_params,
    vol_kernel,
    geo_kernel,
    clear_mask,
):
    devices = lax.axis_size("tile") * lax.axis_size("row")
    blocks = swath_blocks.shape[2]
    width = swath_blocks.shape[3]
    bands = bandpass_offset.shape[1]
    pixels = width // bands
    picks = weight_tiles.shape[0]
    cells = lookup_bin.shape[1]
    mixing = jnp.eye(bands, dtype=jnp.float32)[None, :, :] + bandpass_offset
    target = footprint.reshape(blocks)
    tag = (
        tile_pick.reshape(blocks) * 2 + sensor.reshape(blocks)
    ) * cells + cell_row.reshape(blocks)
    number = jnp.arange(blocks, dtype=jnp.int32)
    same = target[:, None] == target[None, :]
    earlier = number[:, None] > number[None, :]
    rank = jnp.sum(jnp.logical_and(same, earlier).astype(jnp.int32), axis=1)
    position = slot_of(target, rank, devices // CHUNKS)
    codes = picks * 2 * cells
    smem = pl.BlockSpec(memory_space=pltpu.SMEM)
    vmem = pl.BlockSpec(memory_space=pltpu.VMEM)
    f32 = jnp.float32
    result = pl.pallas_call(
        kernel,
        out_shape=jax.ShapeDtypeStruct((cells, width), jnp.bfloat16),
        in_specs=[smem] * 3 + [vmem] * 9,
        out_specs=vmem,
        scratch_shapes=[
            pltpu.VMEM((devices, 2 * bands, pixels), jnp.bfloat16),
            pltpu.VMEM((devices, 2 * bands, pixels), jnp.bfloat16),
            pltpu.VMEM((devices, 1, 128), jnp.int32),
            pltpu.VMEM((devices, 1, 128), jnp.int32),
            pltpu.VMEM((pixels // HALF * devices // CHUNKS * 2 * bands, HALF), f32),
            pltpu.VMEM((codes, width), f32),
            pltpu.VMEM((2 * cells, width), f32),
            pltpu.VMEM((cells + 16, width), f32),
            pltpu.VMEM((cells, width), f32),
            pltpu.VMEM((2, 1, width), f32),
            pltpu.VMEM((2, 1, width), f32),
            pltpu.SemaphoreType.DMA,
            pltpu.SemaphoreType.DMA((CHUNKS,)),
            pltpu.SemaphoreType.DMA,
            pltpu.SemaphoreType.DMA((CHUNKS,)),
            pltpu.SemaphoreType.DMA((2,)),
            pltpu.SemaphoreType.DMA((2,)),
        ],
        compiler_params=pltpu.CompilerParams(
            has_side_effects=True, vmem_limit_bytes=56 * 1024 * 1024
        ),
    )(
        mixing.reshape(2, bands * bands),
        lookup_table,
        brdf_params,
        swath_blocks.reshape(blocks, width),
        position.reshape(1, blocks),
        tag.reshape(1, blocks),
        weight_tiles,
        lookup_bin[0],
        lookup_frac[0],
        vol_kernel[0],
        geo_kernel[0],
        clear_mask[0],
    )
    return result[None]


def solution(mesh):
    in_specs = (
        P("tile", "row", None, None),
        P("tile", "row", None, None),
        P("tile", "row", None),
        P("tile", "row", None),
        P("tile", "row", None),
        P(),
        P(),
        P(),
        P("tile", "row", None),
        P("tile", "row", None),
        P(),
        P("tile", "row", None),
        P("tile", "row", None),
        P("tile", "row", None),
    )
    return jax.shard_map(
        on_device, mesh=mesh, in_specs=in_specs, out_specs=P("tile", "row", None), check_vma=False
    )
```

time: 386 us -> 154 us (0.40)
  the two profiles are of different devices: /device:TPU:70 before, /device:TPU:1 now
where the time goes in v1:
time: 154 us
  Pallas kernels  145 us (94%)
  other arithmetic  4.51 us (3%)
  local copies, waits for them, and re-layouts  3.89 us (3%)
    pallas_call x1, Pallas kernels, on_device(): pl.pallas_call(kernel, out_shape=jax.ShapeDtypeStruct((cells, width), jnp...  145 us
    unnamed x2, local copies, waits for them, and re-layouts  3.23 us

profile of v1, /device:TPU:1, one launch (start us, length us, event | category | flops | bytes accessed | tf_op | source)
XLA Modules:
  0.0 153.6 jit_solution(2070832410068270923)
XLA Ops:
  0.0 1.3 add_bitcast_fusion.code_ref
  1.3 1.3 copy.16.brdf_ref
  2.7 0.7 reduce
  3.4 0.4 convert_reduce_fusion
  3.7 1.4 fusion.4.position_ref
  5.2 0.7 broadcast_add_fusion
  5.9 0.7 reshape.599.mixing_ref
  6.5 145.1 %shard_map.136 = bf16[128,2048]{1,0:T(8,128)(2,1)} custom-call(f32[2,64]{1,0:T(2,128)} %reshape.599.mixing_ref, f32[8,33]{1,0:T(8,128)} %table_ref.1, f32[8,3]{1,0:T(8,128)} %copy.16.brdf_ref, bf16[768,2048]{1,0:T(8,128)(2,1)} %bitcast.24, s32[1,768]{1,0:T(1,128)} %fusion.4.position_ref, s32[1,768]{1,0:T(1,128)} %add_bitcast_fusion.code_ref, ...), custom_call_target="tpu_custom_call" | custom-call | tf_op jit(solution)/shard_map/pallas_call | solution.py:291
  151.7 1.9 %copy.18 = bf16[1,128,2048]{2,1,0:T(8,128)(2,1)} copy(bf16[1,128,2048]{2,1,0:T(8,128)(2,1)} %bitcast.25) | data formatting | bytes 1048576
  (1 shorter events, 0.0 us)

commit v2 on v1

v2 whole, which is shorter than its diff:
```python
import jax
import jax.numpy as jnp
from jax import lax
from jax.experimental import pallas as pl
from jax.experimental.pallas import tpu as pltpu
from jax.sharding import PartitionSpec as P

nadir_volume = 0.3
nadir_geometric = 0.6
MESH = pl.DeviceIdType.MESH
RING = 8
PEERS = 64
SLOTS = 16
HALF = 128
STREAMS = [(plan, pair, sign) for pair in range(2) for plan in range(2) for sign in (1, -1)]


def hops(pair, sign):
    return 4 if (pair == 0) == (sign > 0) else 3


def kernel(
    offset_ref,
    table_ref,
    brdf_ref,
    blocks_ref,
    target_ref,
    cell_ref,
    pick_ref,
    sensor_ref,
    weights_ref,
    bin_ref,
    frac_ref,
    vol_ref,
    geo_ref,
    mask_ref,
    out_ref,
    traits,
    spread,
    choose_out,
    choose_in,
    outgoing,
    incoming,
    tags_out,
    tags_in,
    sums,
    ring_out,
    ring_in,
    grid,
    factor,
    edge_out,
    edge_in,
    send_sem,
    recv_sem,
    tag_send_sem,
    tag_recv_sem,
    ring_send_sem,
    ring_recv_sem,
    edge_send_sem,
    edge_recv_sem,
):
    blocks = blocks_ref.shape[0]
    bands = 8
    pixels = 256
    cells = out_ref.shape[0]
    picks = weights_ref.shape[0] // pixels
    f32, bf16, i32 = jnp.float32, jnp.bfloat16, jnp.int32
    tile = lax.axis_index("tile")
    row = lax.axis_index("row")
    z, x, core = tile // 8, (tile // 2) % 4, tile % 2
    place = (row, z)

    def peer(plan, t):
        step = t % RING
        other = (t // RING + t) % RING
        side = ((x + other // 2) % 4) * 2 + (core + other % 2) % 2
        if plan == 0:
            return ((z + step) % 8) * 8 + side, row
        return z * 8 + side, (row + step) % 8

    target = target_ref[...]
    joined = ((target * 8 + pick_ref[...] * 2 + sensor_ref[...])).astype(f32)
    for j in range(blocks // 128):
        part = jnp.broadcast_to(joined[:, j * 128 : (j + 1) * 128], (128, 128))
        traits[pl.ds(j * 128, 128), :] = jnp.transpose(part).astype(i32)
    rank_parts = []
    own_target = traits[...] >> 3
    first = lax.broadcasted_iota(i32, (blocks, 128), 0)
    for j in range(blocks // 128):
        second = lax.broadcasted_iota(i32, (blocks, 128), 1) + j * 128
        same = (own_target == target[:, j * 128 : (j + 1) * 128]) & (first < second)
        rank_parts.append(jnp.sum(same.astype(f32), axis=0, keepdims=True))
    rank = jnp.concatenate(rank_parts, axis=1).astype(i32)

    to_row = target & 7
    to_z = target >> 6
    to_x = (target >> 4) & 3
    to_core = (target >> 3) & 1
    other = ((to_x - x) & 3) * 2 + ((to_core - core) & 1)
    for plan in range(2):
        step = ((to_z - z) & 7) if plan == 0 else ((to_row - row) & 7)
        number = ((other - step) & 7) * 8 + step
        slot = (to_row if plan == 0 else to_z) * 2 + rank
        position = number * SLOTS + slot
        for i in range(PEERS * SLOTS // 128):
            here = lax.broadcasted_iota(i32, (128, blocks), 0) + i * 128
            choose_out[plan, pl.ds(i * 128, 128), :] = (position == here).astype(f32).astype(bf16)
        to_peer = (lax.broadcasted_iota(i32, (PEERS, blocks), 0) == number).astype(f32).astype(bf16)
        lane_slot = lax.broadcasted_iota(i32, (128, blocks), 0) & (SLOTS - 1)
        marks = jnp.where(lane_slot == slot, cell_ref[...] + 1, 0).astype(f32).astype(bf16)
        found = lax.dot_general(
            to_peer, marks, (((1,), (1,)), ((), ())), preferred_element_type=f32
        )
        lane = lax.broadcasted_iota(i32, (PEERS, 128), 1) & (SLOTS - 1)
        base = ((lane >> 1) * cells - 1).astype(f32)
        tags_out[plan] = jnp.where(found > 0.0, base + found, -1.0).reshape(PEERS, 1, 128)
        tags_in[plan, 0] = tags_out[plan, 0]

    @pl.loop(1, PEERS)
    def _(t):
        for plan in range(2):
            pltpu.make_async_remote_copy(
                src_ref=tags_out.at[plan, t],
                dst_ref=tags_in.at[plan, t],
                send_sem=tag_send_sem.at[plan],
                recv_sem=tag_recv_sem.at[plan],
                device_id=peer(plan, t),
                device_id_type=MESH,
            ).start()

    for first_band in range(4):
        pair_bands = (first_band, first_band + 4)

        @pl.loop(0, blocks // 64)
        def _(g):
            rows = pl.ds(pl.multiple_of(g * 64, 64), 64)
            trait = traits[rows, :]
            is_second = (trait & 1) == 1
            pick = (trait >> 1) & 3
            for h in range(pixels // HALF):
                totals = [None, None]
                for other in range(bands):
                    value = blocks_ref[rows, pl.ds(other * pixels + h * HALF, HALF)].astype(f32)
                    for plan in range(2):
                        band = pair_bands[plan]
                        own = 1.0 if band == other else 0.0
                        mix = jnp.where(
                            is_second,
                            own + offset_ref[1, band, other],
                            own + offset_ref[0, band, other],
                        )
                        term = mix * value
                        totals[plan] = term if other == 0 else totals[plan] + term
                for plan in range(2):
                    for k in range(picks):
                        spread[plan, rows, pl.ds(k * pixels + h * HALF, HALF)] = jnp.where(
                            pick == k, totals[plan], 0.0
                        ).astype(bf16)

        for plan in range(2):
            band = pair_bands[plan]
            resampled = jnp.dot(
                spread[plan], weights_ref[...], preferred_element_type=f32
            ).astype(bf16)
            moved = jnp.dot(choose_out[plan], resampled, preferred_element_type=f32)
            outgoing[band] = moved.astype(bf16).reshape(PEERS, SLOTS, pixels)
            incoming[band, 0] = outgoing[band, 0]

        @pl.loop(1, PEERS)
        def _(t):
            for plan in range(2):
                band = pair_bands[plan]
                pltpu.make_async_remote_copy(
                    src_ref=outgoing.at[band, t],
                    dst_ref=incoming.at[band, t],
                    send_sem=send_sem.at[band],
                    recv_sem=recv_sem.at[band],
                    device_id=peer(plan, t),
                    device_id_type=MESH,
                ).start()

    bins = table_ref.shape[1] - 1

    @pl.loop(0, cells // 8)
    def _(g):
        rows = pl.ds(pl.multiple_of(g * 8, 8), 8)
        which = bin_ref[rows, :]
        part = frac_ref[rows, :]
        volume_angle = vol_ref[rows, :]
        geometric_angle = geo_ref[rows, :]
        keep = mask_ref[rows, :].astype(f32)
        lower = [jnp.full((8, pixels), table_ref[b, 0]) for b in range(bands)]
        upper = [jnp.full((8, pixels), table_ref[b, 1]) for b in range(bands)]
        for n in range(1, bins):
            here = which == n
            for b in range(bands):
                lower[b] = jnp.where(here, table_ref[b, n], lower[b])
                upper[b] = jnp.where(here, table_ref[b, n + 1], upper[b])
        for b in range(bands):
            value = lower[b] * (1.0 - part) + upper[b] * part
            isotropic, volume, geometric = brdf_ref[0, b], brdf_ref[1, b], brdf_ref[2, b]
            numerator = isotropic + volume * nadir_volume + geometric * nadir_geometric
            denominator = isotropic + volume * volume_angle + geometric * geometric_angle
            factor[rows, pl.ds(b * pixels, pixels)] = value * (numerator / denominator) * keep

    rest = pl.ds(1, PEERS - 1)
    sublane = lax.broadcasted_iota(i32, (8, 128), 0)
    lane_group = lax.broadcasted_iota(i32, (8, 128), 1) >> 4
    line = lax.broadcasted_iota(i32, (RING * cells, 128), 0).astype(f32)
    for plan in range(2):
        pltpu.make_async_copy(
            tags_in.at[plan, rest], tags_in.at[plan, rest], tag_recv_sem.at[plan]
        ).wait()
        arrived = tags_in[plan].reshape(PEERS, 128)
        for g in range(PEERS // 8):
            code = jnp.sum(
                jnp.where(sublane == lane_group, arrived[g * 8 : (g + 1) * 8], 0.0),
                axis=0,
                keepdims=True,
            )
            choose_in[plan, :, pl.ds(g * 128, 128)] = (line == code).astype(f32).astype(bf16)

    def gather_pair(plan, pair):
        for band in (plan * 4 + pair * 2, plan * 4 + pair * 2 + 1):
            pltpu.make_async_copy(
                incoming.at[band, rest], incoming.at[band, rest], recv_sem.at[band]
            ).wait()
            sums[band] = jnp.dot(
                choose_in[plan],
                incoming[band].reshape(PEERS * SLOTS, pixels),
                preferred_element_type=f32,
            )

    def ring_copy(plan, pair, sign, step):
        stream = STREAMS.index((plan, pair, sign))
        if plan == 0:
            device = (tile, (row + sign + 8) % 8)
        else:
            device = (((z + sign + 8) % 8) * 8 + x * 2 + core, row)
        return pltpu.make_async_remote_copy(
            src_ref=ring_out.at[stream, step],
            dst_ref=ring_in.at[stream, step],
            send_sem=ring_send_sem.at[stream, step],
            recv_sem=ring_recv_sem.at[stream, step],
            device_id=device,
            device_id_type=MESH,
        )

    def ring_step(pair, step):
        for plan in range(2):
            if step == 0:
                gather_pair(plan, pair)
            for sign in (1, -1):
                length = hops(pair, sign)
                if step >= length:
                    continue
                stream = STREAMS.index((plan, pair, sign))
                toward = (place[plan] + sign * (length - step) + 8) % 8
                lines = pl.ds(pl.multiple_of(toward * cells, cells), cells)
                if step > 0:
                    ring_copy(plan, pair, sign, step - 1).wait_recv()
                for i in range(2):
                    value = sums[plan * 4 + pair * 2 + i, lines, :]
                    if step > 0:
                        value = value + ring_in[stream, step - 1, i].astype(f32)
                    ring_out[stream, step, i] = value.astype(bf16)
                ring_copy(plan, pair, sign, step).start()

    def finish(pair):
        for plan in range(2):
            lines = pl.ds(pl.multiple_of(place[plan] * cells, cells), cells)
            for sign in (1, -1):
                ring_copy(plan, pair, sign, hops(pair, sign) - 1).wait_recv()
            for i in range(2):
                band = plan * 4 + pair * 2 + i
                total = sums[band, lines, :]
                for sign in (1, -1):
                    stream = STREAMS.index((plan, pair, sign))
                    total = total + ring_in[stream, hops(pair, sign) - 1, i].astype(f32)
                grid[pl.ds(8, cells), pl.ds(band * pixels, pixels)] = total

    ring_step(0, 0)
    ring_step(0, 1)
    ring_step(1, 0)
    ring_step(0, 2)
    ring_step(1, 1)
    ring_step(0, 3)
    ring_step(1, 2)
    finish(0)
    ring_step(1, 3)
    finish(1)

    edge_out[0] = grid[pl.ds(8 + cells - 1, 1), :]
    edge_out[1] = grid[pl.ds(8, 1), :]
    copies = [
        pltpu.make_async_remote_copy(
            src_ref=edge_out.at[side],
            dst_ref=edge_in.at[side],
            send_sem=edge_send_sem.at[side],
            recv_sem=edge_recv_sem.at[side],
            device_id=(tile, (row + step) % 8),
            device_id_type=MESH,
        )
        for side, step in ((0, 1), (1, 7))
    ]
    for copy in copies:
        copy.start()
    for plan in range(2):
        pltpu.make_async_copy(
            tags_out.at[plan, rest], tags_out.at[plan, rest], tag_send_sem.at[plan]
        ).wait()
    for band in range(bands):
        pltpu.make_async_copy(
            outgoing.at[band, rest], outgoing.at[band, rest], send_sem.at[band]
        ).wait()
    for plan, pair, sign in STREAMS:
        for step in range(hops(pair, sign)):
            ring_copy(plan, pair, sign, step).wait_send()
    for copy in copies:
        copy.wait()
    grid[pl.ds(7, 1), :] = jnp.where(row == 0, 0.0, edge_in[0])
    grid[pl.ds(8 + cells, 1), :] = jnp.where(row == 7, 0.0, edge_in[1])
    for g in range(cells // 16):
        above = grid[pl.ds(g * 16 + 7, 16), :]
        here = grid[pl.ds(g * 16 + 8, 16), :]
        below = grid[pl.ds(g * 16 + 9, 16), :]
        smoothed = 0.25 * above + 0.5 * here + 0.25 * below
        rows = pl.ds(g * 16, 16)
        out_ref[rows, :] = (smoothed * factor[rows, :]).astype(bf16)


def on_device(
    swath_blocks,
    footprint,
    cell_row,
    tile_pick,
    sensor,
    bandpass_offset,
    weight_tiles,
    lookup_table,
    lookup_bin,
    lookup_frac,
    brdf_params,
    vol_kernel,
    geo_kernel,
    clear_mask,
):
    blocks = swath_blocks.shape[2]
    width = swath_blocks.shape[3]
    bands = bandpass_offset.shape[1]
    pixels = width // bands
    picks = weight_tiles.shape[0]
    cells = lookup_bin.shape[1]
    smem = pl.BlockSpec(memory_space=pltpu.SMEM)
    vmem = pl.BlockSpec(memory_space=pltpu.VMEM)
    f32, bf16 = jnp.float32, jnp.bfloat16
    dma = pltpu.SemaphoreType.DMA
    result = pl.pallas_call(
        kernel,
        out_shape=jax.ShapeDtypeStruct((cells, width), bf16),
        in_specs=[smem] * 3 + [vmem] * 11,
        out_specs=vmem,
        scratch_shapes=[
            pltpu.VMEM((blocks, 128), jnp.int32),
            pltpu.VMEM((2, blocks, picks * pixels), bf16),
            pltpu.VMEM((2, PEERS * SLOTS, blocks), bf16),
            pltpu.VMEM((2, RING * cells, PEERS * SLOTS), bf16),
            pltpu.VMEM((bands, PEERS, SLOTS, pixels), bf16),
            pltpu.VMEM((bands, PEERS, SLOTS, pixels), bf16),
            pltpu.VMEM((2, PEERS, 1, 128), f32),
            pltpu.VMEM((2, PEERS, 1, 128), f32),
            pltpu.VMEM((bands, RING * cells, pixels), f32),
            pltpu.VMEM((len(STREAMS), 4, 2, cells, pixels), bf16),
            pltpu.VMEM((len(STREAMS), 4, 2, cells, pixels), bf16),
            pltpu.VMEM((cells + 16, width), f32),
            pltpu.VMEM((cells, width), f32),
            pltpu.VMEM((2, 1, width), f32),
            pltpu.VMEM((2, 1, width), f32),
            dma((bands,)),
            dma((bands,)),
            dma((2,)),
            dma((2,)),
            dma((len(STREAMS), 4)),
            dma((len(STREAMS), 4)),
            dma((2,)),
            dma((2,)),
        ],
        compiler_params=pltpu.CompilerParams(
            has_side_effects=True, vmem_limit_bytes=58 * 1024 * 1024
        ),
    )(
        bandpass_offset,
        lookup_table,
        brdf_params.T,
        swath_blocks.reshape(blocks, width),
        footprint.reshape(1, blocks),
        cell_row.reshape(1, blocks),
        tile_pick.reshape(1, blocks),
        sensor.reshape(1, blocks),
        weight_tiles.reshape(picks * pixels, pixels),
        lookup_bin[0],
        lookup_frac[0],
        vol_kernel[0],
        geo_kernel[0],
        clear_mask[0],
    )
    return result[None]


def solution(mesh):
    in_specs = (
        P("tile", "row", None, None),
        P("tile", "row", None, None),
        P("tile", "row", None),
        P("tile", "row", None),
        P("tile", "row", None),
        P(),
        P(),
        P(),
        P("tile", "row", None),
        P("tile", "row", None),
        P(),
        P("tile", "row", None),
        P("tile", "row", None),
        P("tile", "row", None),
    )
    return jax.shard_map(
        on_device, mesh=mesh, in_specs=in_specs, out_specs=P("tile", "row", None), check_vma=False
    )
```

time: 154 us -> 118 us (0.77)
  the two profiles are of different devices: /device:TPU:1 before, /device:TPU:2 now
where the time goes in v2:
time: 118 us
  Pallas kernels  116 us (98%)
  local copies, waits for them, and re-layouts  1.88 us (2%)
    pallas_call x1, Pallas kernels, on_device(): pl.pallas_call(kernel, out_shape=jax.ShapeDtypeStruct((cells, width), bf1...  116 us

profile of v2, /device:TPU:2, one launch (start us, length us, event | category | flops | bytes accessed | tf_op | source)
XLA Modules:
  0.0 117.8 jit_solution(8428887784995302657)
XLA Ops:
  0.0 115.9 %shard_map.136 = bf16[128,2048]{1,0:T(8,128)(2,1)} custom-call(f32[2,8,8]{2,1,0:T(8,128)} %offset_ref.1, f32[8,33]{1,0:T(8,128)} %table_ref.1, f32[3,8]{1,0:T(4,128)} %bitcast.25, bf16[768,2048]{1,0:T(8,128)(2,1)} %bitcast.13, s32[1,768]{1,0:T(1,128)} %bitcast.21, s32[1,768]{1,0:T(1,128)} %bitcast.22, s32[1,768]{1,0:T(1,128)} %bitcast.23, ...), custom_call_target="tpu_custom_call" | custom-call | tf_op jit(solution)/shard_map/pallas_call | solution.py:358
  115.9 1.9 %copy.16 = bf16[1,128,2048]{2,1,0:T(8,128)(2,1)} copy(bf16[1,128,2048]{2,1,0:T(8,128)(2,1)} %bitcast.14) | data formatting | bytes 1048576

commit v3 on v2

--- a/solution.py
+++ b/solution.py
@@ -58,6 +58,7 @@
     ring_recv_sem,
     edge_send_sem,
     edge_recv_sem,
+    beside_sem,
 ):
     blocks = blocks_ref.shape[0]
     bands = 8
@@ -77,6 +78,16 @@
         if plan == 0:
             return ((z + step) % 8) * 8 + side, row
         return z * 8 + side, (row + step) % 8
+
+    around = pltpu.get_barrier_semaphore()
+    for step in range(1, 8):
+        side = ((x + step // 2) % 4) * 2 + (core + step % 2) % 2
+        for device in (
+            (((z + step) % 8) * 8 + x * 2 + core, row),
+            (tile, (row + step) % 8),
+            (z * 8 + side, row),
+        ):
+            pl.semaphore_signal(around, inc=1, device_id=device, device_id_type=MESH)
 
     target = target_ref[...]
     joined = ((target * 8 + pick_ref[...] * 2 + sensor_ref[...])).astype(f32)
@@ -116,17 +127,12 @@
         tags_out[plan] = jnp.where(found > 0.0, base + found, -1.0).reshape(PEERS, 1, 128)
         tags_in[plan, 0] = tags_out[plan, 0]
 
-    @pl.loop(1, PEERS)
-    def _(t):
-        for plan in range(2):
-            pltpu.make_async_remote_copy(
-                src_ref=tags_out.at[plan, t],
-                dst_ref=tags_in.at[plan, t],
-                send_sem=tag_send_sem.at[plan],
-                recv_sem=tag_recv_sem.at[plan],
-                device_id=peer(plan, t),
-                device_id_type=MESH,
-            ).start()
+    pl.semaphore_wait(around, 21)
+    for step in range(1, 8):
+        side = ((x + step // 2) % 4) * 2 + (core + step % 2) % 2
+        pl.semaphore_signal(
+            beside_sem, inc=1, device_id=(z * 8 + side, row), device_id_type=MESH
+        )
 
     for first_band in range(4):
         pair_bands = (first_band, first_band + 4)
@@ -166,6 +172,9 @@
             outgoing[band] = moved.astype(bf16).reshape(PEERS, SLOTS, pixels)
             incoming[band, 0] = outgoing[band, 0]
 
+        if first_band == 0:
+            pl.semaphore_wait(beside_sem, 7)
+
         @pl.loop(1, PEERS)
         def _(t):
             for plan in range(2):
@@ -178,6 +187,20 @@
                     device_id=peer(plan, t),
                     device_id_type=MESH,
                 ).start()
+
+        if first_band == 0:
+
+            @pl.loop(1, PEERS)
+            def _(t):
+                for plan in range(2):
+                    pltpu.make_async_remote_copy(
+                        src_ref=tags_out.at[plan, t],
+                        dst_ref=tags_in.at[plan, t],
+                        send_sem=tag_send_sem.at[plan],
+                        recv_sem=tag_recv_sem.at[plan],
+                        device_id=peer(plan, t),
+                        device_id_type=MESH,
+                    ).start()
 
     bins = table_ref.shape[1] - 1
 
@@ -384,9 +407,10 @@
             dma((len(STREAMS), 4)),
             dma((2,)),
             dma((2,)),
+            pltpu.SemaphoreType.REGULAR,
         ],
         compiler_params=pltpu.CompilerParams(
-            has_side_effects=True, vmem_limit_bytes=58 * 1024 * 1024
+            has_side_effects=True, collective_id=0, vmem_limit_bytes=58 * 1024 * 1024
         ),
     )(
         bandpass_offset,

time: 118 us -> 104 us (0.88)
  the two profiles are of different devices: /device:TPU:2 before, /device:TPU:4 now
where the time goes in v3:
time: 104 us; the launch traced here: 103 us
  Pallas kernels  101 us (97%)
  local copies, waits for them, and re-layouts  1.88 us (2%)
    pallas_call x1, Pallas kernels, on_device(): pl.pallas_call(kernel, out_shape=jax.ShapeDtypeStruct((cells, width), bf1...  101 us

profile of v3, /device:TPU:4, one launch (start us, length us, event | category | flops | bytes accessed | tf_op | source)
XLA Modules:
  0.0 103.4 jit_solution(1606433633423202779)
XLA Ops:
  0.0 101.5 %shard_map.136 = bf16[128,2048]{1,0:T(8,128)(2,1)} custom-call(f32[2,8,8]{2,1,0:T(8,128)} %offset_ref.1, f32[8,33]{1,0:T(8,128)} %table_ref.1, f32[3,8]{1,0:T(4,128)} %bitcast.25, bf16[768,2048]{1,0:T(8,128)(2,1)} %bitcast.13, s32[1,768]{1,0:T(1,128)} %bitcast.21, s32[1,768]{1,0:T(1,128)} %bitcast.22, s32[1,768]{1,0:T(1,128)} %bitcast.23, ...), custom_call_target="tpu_custom_call" | custom-call | tf_op jit(solution)/shard_map/pallas_call | solution.py:381
  101.5 1.9 %copy.16 = bf16[1,128,2048]{2,1,0:T(8,128)(2,1)} copy(bf16[1,128,2048]{2,1,0:T(8,128)(2,1)} %bitcast.14) | data formatting | bytes 1048576

commit v4 on v3

--- a/solution.py
+++ b/solution.py
@@ -23,18 +23,25 @@
     offset_ref,
     table_ref,
     brdf_ref,
-    blocks_ref,
+    blocks_hbm,
     target_ref,
     cell_ref,
     pick_ref,
     sensor_ref,
+    weights_hbm,
+    bin_hbm,
+    frac_hbm,
+    vol_hbm,
+    geo_hbm,
+    mask_hbm,
+    out_ref,
+    blocks_ref,
     weights_ref,
     bin_ref,
     frac_ref,
     vol_ref,
     geo_ref,
     mask_ref,
-    out_ref,
     traits,
     spread,
     choose_out,
@@ -59,6 +66,7 @@
     edge_send_sem,
     edge_recv_sem,
     beside_sem,
+    load_sem,
 ):
     blocks = blocks_ref.shape[0]
     bands = 8
@@ -88,6 +96,22 @@
             (z * 8 + side, row),
         ):
             pl.semaphore_signal(around, inc=1, device_id=device, device_id_type=MESH)
+    loads = [
+        pltpu.make_async_copy(source, kept, load_sem.at[i])
+        for i, (source, kept) in enumerate(
+            (
+                (blocks_hbm, blocks_ref),
+                (weights_hbm, weights_ref),
+                (bin_hbm, bin_ref),
+                (frac_hbm, frac_ref),
+                (vol_hbm, vol_ref),
+                (geo_hbm, geo_ref),
+                (mask_hbm, mask_ref),
+            )
+        )
+    ]
+    for load in loads:
+        load.start()
 
     target = target_ref[...]
     joined = ((target * 8 + pick_ref[...] * 2 + sensor_ref[...])).astype(f32)
@@ -108,6 +132,7 @@
     to_x = (target >> 4) & 3
     to_core = (target >> 3) & 1
     other = ((to_x - x) & 3) * 2 + ((to_core - core) & 1)
+    numbers, slots = [], []
     for plan in range(2):
         step = ((to_z - z) & 7) if plan == 0 else ((to_row - row) & 7)
         number = ((other - step) & 7) * 8 + step
@@ -116,16 +141,8 @@
         for i in range(PEERS * SLOTS // 128):
             here = lax.broadcasted_iota(i32, (128, blocks), 0) + i * 128
             choose_out[plan, pl.ds(i * 128, 128), :] = (position == here).astype(f32).astype(bf16)
-        to_peer = (lax.broadcasted_iota(i32, (PEERS, blocks), 0) == number).astype(f32).astype(bf16)
-        lane_slot = lax.broadcasted_iota(i32, (128, blocks), 0) & (SLOTS - 1)
-        marks = jnp.where(lane_slot == slot, cell_ref[...] + 1, 0).astype(f32).astype(bf16)
-        found = lax.dot_general(
-            to_peer, marks, (((1,), (1,)), ((), ())), preferred_element_type=f32
-        )
-        lane = lax.broadcasted_iota(i32, (PEERS, 128), 1) & (SLOTS - 1)
-        base = ((lane >> 1) * cells - 1).astype(f32)
-        tags_out[plan] = jnp.where(found > 0.0, base + found, -1.0).reshape(PEERS, 1, 128)
-        tags_in[plan, 0] = tags_out[plan, 0]
+        numbers.append(number)
+        slots.append(slot)
 
     pl.semaphore_wait(around, 21)
     for step in range(1, 8):
@@ -134,6 +151,8 @@
             beside_sem, inc=1, device_id=(z * 8 + side, row), device_id_type=MESH
         )
 
+    loads[0].wait()
+    loads[1].wait()
     for first_band in range(4):
         pair_bands = (first_band, first_band + 4)
 
@@ -189,6 +208,17 @@
                 ).start()
 
         if first_band == 0:
+            for plan in range(2):
+                to_peer = (lax.broadcasted_iota(i32, (PEERS, blocks), 0) == numbers[plan]).astype(f32).astype(bf16)
+                lane_slot = lax.broadcasted_iota(i32, (128, blocks), 0) & (SLOTS - 1)
+                marks = jnp.where(lane_slot == slots[plan], cell_ref[...] + 1, 0).astype(f32).astype(bf16)
+                found = lax.dot_general(
+                    to_peer, marks, (((1,), (1,)), ((), ())), preferred_element_type=f32
+                )
+                lane = lax.broadcasted_iota(i32, (PEERS, 128), 1) & (SLOTS - 1)
+                base = ((lane >> 1) * cells - 1).astype(f32)
+                tags_out[plan] = jnp.where(found > 0.0, base + found, -1.0).reshape(PEERS, 1, 128)
+                tags_in[plan, 0] = tags_out[plan, 0]
 
             @pl.loop(1, PEERS)
             def _(t):
@@ -202,6 +232,122 @@
                         device_id_type=MESH,
                     ).start()
 
+    rest = pl.ds(1, PEERS - 1)
+    sublane = lax.broadcasted_iota(i32, (8, 128), 0)
+    lane_group = lax.broadcasted_iota(i32, (8, 128), 1) >> 4
+    line = lax.broadcasted_iota(i32, (RING * cells, 128), 0).astype(f32)
+    for plan in range(2):
+        pltpu.make_async_copy(
+            tags_in.at[plan, rest], tags_in.at[plan, rest], tag_recv_sem.at[plan]
+        ).wait()
+        arrived = tags_in[plan].reshape(PEERS, 128)
+        for g in range(PEERS // 8):
+            code = jnp.sum(
+                jnp.where(sublane == lane_group, arrived[g * 8 : (g + 1) * 8], 0.0),
+                axis=0,
+                keepdims=True,
+            )
+            choose_in[plan, :, pl.ds(g * 128, 128)] = (line == code).astype(f32).astype(bf16)
+
+    def gather_pair(plan, pair):
+        for band in (plan * 4 + pair * 2, plan * 4 + pair * 2 + 1):
+            pltpu.make_async_copy(
+                incoming.at[band, rest], incoming.at[band, rest], recv_sem.at[band]
+            ).wait()
+            sums[band] = jnp.dot(
+                choose_in[plan],
+                incoming[band].reshape(PEERS * SLOTS, pixels),
+                preferred_element_type=f32,
+            )
+
+    def ring_copy(plan, pair, sign, step):
+        stream = STREAMS.index((plan, pair, sign))
+        if plan == 0:
+            device = (tile, (row + sign + 8) % 8)
+        else:
+            device = (((z + sign + 8) % 8) * 8 + x * 2 + core, row)
+        return pltpu.make_async_remote_copy(
+            src_ref=ring_out.at[stream, step],
+            dst_ref=ring_in.at[stream, step],
+            send_sem=ring_send_sem.at[stream, step],
+            recv_sem=ring_recv_sem.at[stream, step],
+            device_id=device,
+            device_id_type=MESH,
+        )
+
+    def ring_step(pair, step):
+        for plan in range(2):
+            if step == 0:
+                gather_pair(plan, pair)
+            for sign in (1, -1):
+                length = hops(pair, sign)
+                if step >= length:
+                    continue
+                stream = STREAMS.index((plan, pair, sign))
+                toward = (place[plan] + sign * (length - step) + 8) % 8
+                lines = pl.ds(pl.multiple_of(toward * cells, cells), cells)
+                if step > 0:
+                    ring_copy(plan, pair, sign, step - 1).wait_recv()
+                for i in range(2):
+                    value = sums[plan * 4 + pair * 2 + i, lines, :]
+                    if step > 0:
+                        value = value + ring_in[stream, step - 1, i].astype(f32)
+                    ring_out[stream, step, i] = value.astype(bf16)
+                ring_copy(plan, pair, sign, step).start()
+
+    def finish(pair):
+        for plan in range(2):
+            lines = pl.ds(pl.multiple_of(place[plan] * cells, cells), cells)
+            for sign in (1, -1):
+                ring_copy(plan, pair, sign, hops(pair, sign) - 1).wait_recv()
+            for i in range(2):
+                band = plan * 4 + pair * 2 + i
+                total = sums[band, lines, :]
+                for sign in (1, -1):
+                    stream = STREAMS.index((plan, pair, sign))
+                    total = total + ring_in[stream, hops(pair, sign) - 1, i].astype(f32)
+                grid[pl.ds(8, cells), pl.ds(band * pixels, pixels)] = total
+
+    span = 2 * pixels
+
+    def edge_copy(pair, side):
+        return pltpu.make_async_remote_copy(
+            src_ref=edge_out.at[pair, side],
+            dst_ref=edge_in.at[pair, side],
+            send_sem=edge_send_sem.at[pair, side],
+            recv_sem=edge_recv_sem.at[pair, side],
+            device_id=(tile, (row + (1, 7)[side]) % 8),
+            device_id_type=MESH,
+        )
+
+    def send_edges(pair):
+        for side, line_at in ((0, 8 + cells - 1), (1, 8)):
+            for plan in range(2):
+                edge_out[pair, side, :, pl.ds(plan * span, span)] = grid[
+                    pl.ds(line_at, 1), pl.ds((plan * 2 + pair) * span, span)
+                ]
+            edge_copy(pair, side).start()
+
+    def smooth(pair):
+        for side in range(2):
+            edge_copy(pair, side).wait()
+        for plan in range(2):
+            lanes = pl.ds((plan * 2 + pair) * span, span)
+            held = pl.ds(plan * span, span)
+            grid[pl.ds(7, 1), lanes] = jnp.where(row == 0, 0.0, edge_in[pair, 0, :, held])
+            grid[pl.ds(8 + cells, 1), lanes] = jnp.where(row == 7, 0.0, edge_in[pair, 1, :, held])
+            for g in range(cells // 16):
+                above = grid[pl.ds(g * 16 + 7, 16), lanes]
+                here = grid[pl.ds(g * 16 + 8, 16), lanes]
+                below = grid[pl.ds(g * 16 + 9, 16), lanes]
+                smoothed = 0.25 * above + 0.5 * here + 0.25 * below
+                rows = pl.ds(g * 16, 16)
+                out_ref[rows, lanes] = (smoothed * factor[rows, lanes]).astype(bf16)
+
+    ring_step(0, 0)
+
+    for load in loads[2:]:
+        load.wait()
     bins = table_ref.shape[1] - 1
 
     @pl.loop(0, cells // 8)
@@ -226,83 +372,6 @@
             denominator = isotropic + volume * volume_angle + geometric * geometric_angle
             factor[rows, pl.ds(b * pixels, pixels)] = value * (numerator / denominator) * keep
 
-    rest = pl.ds(1, PEERS - 1)
-    sublane = lax.broadcasted_iota(i32, (8, 128), 0)
-    lane_group = lax.broadcasted_iota(i32, (8, 128), 1) >> 4
-    line = lax.broadcasted_iota(i32, (RING * cells, 128), 0).astype(f32)
-    for plan in range(2):
-        pltpu.make_async_copy(
-            tags_in.at[plan, rest], tags_in.at[plan, rest], tag_recv_sem.at[plan]
-        ).wait()
-        arrived = tags_in[plan].reshape(PEERS, 128)
-        for g in range(PEERS // 8):
-            code = jnp.sum(
-                jnp.where(sublane == lane_group, arrived[g * 8 : (g + 1) * 8], 0.0),
-                axis=0,
-                keepdims=True,
-            )
-            choose_in[plan, :, pl.ds(g * 128, 128)] = (line == code).astype(f32).astype(bf16)
-
-    def gather_pair(plan, pair):
-        for band in (plan * 4 + pair * 2, plan * 4 + pair * 2 + 1):
-            pltpu.make_async_copy(
-                incoming.at[band, rest], incoming.at[band, rest], recv_sem.at[band]
-            ).wait()
-            sums[band] = jnp.dot(
-                choose_in[plan],
-                incoming[band].reshape(PEERS * SLOTS, pixels),
-                preferred_element_type=f32,
-            )
-
-    def ring_copy(plan, pair, sign, step):
-        stream = STREAMS.index((plan, pair, sign))
-        if plan == 0:
-            device = (tile, (row + sign + 8) % 8)
-        else:
-            device = (((z + sign + 8) % 8) * 8 + x * 2 + core, row)
-        return pltpu.make_async_remote_copy(
-            src_ref=ring_out.at[stream, step],
-            dst_ref=ring_in.at[stream, step],
-            send_sem=ring_send_sem.at[stream, step],
-            recv_sem=ring_recv_sem.at[stream, step],
-            device_id=device,
-            device_id_type=MESH,
-        )
-
-    def ring_step(pair, step):
-        for plan in range(2):
-            if step == 0:
-                gather_pair(plan, pair)
-            for sign in (1, -1):
-                length = hops(pair, sign)
-                if step >= length:
-                    continue
-                stream = STREAMS.index((plan, pair, sign))
-                toward = (place[plan] + sign * (length - step) + 8) % 8
-                lines = pl.ds(pl.multiple_of(toward * cells, cells), cells)
-                if step > 0:
-                    ring_copy(plan, pair, sign, step - 1).wait_recv()
-                for i in range(2):
-                    value = sums[plan * 4 + pair * 2 + i, lines, :]
-                    if step > 0:
-                        value = value + ring_in[stream, step - 1, i].astype(f32)
-                    ring_out[stream, step, i] = value.astype(bf16)
-                ring_copy(plan, pair, sign, step).start()
-
-    def finish(pair):
-        for plan in range(2):
-            lines = pl.ds(pl.multiple_of(place[plan] * cells, cells), cells)
-            for sign in (1, -1):
-                ring_copy(plan, pair, sign, hops(pair, sign) - 1).wait_recv()
-            for i in range(2):
-                band = plan * 4 + pair * 2 + i
-                total = sums[band, lines, :]
-                for sign in (1, -1):
-                    stream = STREAMS.index((plan, pair, sign))
-                    total = total + ring_in[stream, hops(pair, sign) - 1, i].astype(f32)
-                grid[pl.ds(8, cells), pl.ds(band * pixels, pixels)] = total
-
-    ring_step(0, 0)
     ring_step(0, 1)
     ring_step(1, 0)
     ring_step(0, 2)
@@ -310,24 +379,11 @@
     ring_step(0, 3)
     ring_step(1, 2)
     finish(0)
+    send_edges(0)
     ring_step(1, 3)
+    smooth(0)
     finish(1)
-
-    edge_out[0] = grid[pl.ds(8 + cells - 1, 1), :]
-    edge_out[1] = grid[pl.ds(8, 1), :]
-    copies = [
-        pltpu.make_async_remote_copy(
-            src_ref=edge_out.at[side],
-            dst_ref=edge_in.at[side],
-            send_sem=edge_send_sem.at[side],
-            recv_sem=edge_recv_sem.at[side],
-            device_id=(tile, (row + step) % 8),
-            device_id_type=MESH,
-        )
-        for side, step in ((0, 1), (1, 7))
-    ]
-    for copy in copies:
-        copy.start()
+    send_edges(1)
     for plan in range(2):
         pltpu.make_async_copy(
             tags_out.at[plan, rest], tags_out.at[plan, rest], tag_send_sem.at[plan]
@@ -339,17 +395,7 @@
     for plan, pair, sign in STREAMS:
         for step in range(hops(pair, sign)):
             ring_copy(plan, pair, sign, step).wait_send()
-    for copy in copies:
-        copy.wait()
-    grid[pl.ds(7, 1), :] = jnp.where(row == 0, 0.0, edge_in[0])
-    grid[pl.ds(8 + cells, 1), :] = jnp.where(row == 7, 0.0, edge_in[1])
-    for g in range(cells // 16):
-        above = grid[pl.ds(g * 16 + 7, 16), :]
-        here = grid[pl.ds(g * 16 + 8, 16), :]
-        below = grid[pl.ds(g * 16 + 9, 16), :]
-        smoothed = 0.25 * above + 0.5 * here + 0.25 * below
-        rows = pl.ds(g * 16, 16)
-        out_ref[rows, :] = (smoothed * factor[rows, :]).astype(bf16)
+    smooth(1)
 
 
 def on_device(
@@ -376,14 +422,22 @@
     cells = lookup_bin.shape[1]
     smem = pl.BlockSpec(memory_space=pltpu.SMEM)
     vmem = pl.BlockSpec(memory_space=pltpu.VMEM)
+    hbm = pl.BlockSpec(memory_space=pl.ANY)
     f32, bf16 = jnp.float32, jnp.bfloat16
     dma = pltpu.SemaphoreType.DMA
     result = pl.pallas_call(
         kernel,
         out_shape=jax.ShapeDtypeStruct((cells, width), bf16),
-        in_specs=[smem] * 3 + [vmem] * 11,
+        in_specs=[smem] * 3 + [hbm] + [vmem] * 4 + [hbm] * 6,
         out_specs=vmem,
         scratch_shapes=[
+            pltpu.VMEM((blocks, width), bf16),
+            pltpu.VMEM((picks * pixels, pixels), bf16),
+            pltpu.VMEM((cells, pixels), jnp.int32),
+            pltpu.VMEM((cells, pixels), f32),
+            pltpu.VMEM((cells, pixels), f32),
+            pltpu.VMEM((cells, pixels), f32),
+            pltpu.VMEM((cells, pixels), jnp.int32),
             pltpu.VMEM((blocks, 128), jnp.int32),
             pltpu.VMEM((2, blocks, picks * pixels), bf16),
             pltpu.VMEM((2, PEERS * SLOTS, blocks), bf16),
@@ -397,17 +451,18 @@
             pltpu.VMEM((len(STREAMS), 4, 2, cells, pixels), bf16),
             pltpu.VMEM((cells + 16, width), f32),
             pltpu.VMEM((cells, width), f32),
-            pltpu.VMEM((2, 1, width), f32),
-            pltpu.VMEM((2, 1, width), f32),
+            pltpu.VMEM((2, 2, 1, width // 2), f32),
+            pltpu.VMEM((2, 2, 1, width // 2), f32),
             dma((bands,)),
             dma((bands,)),
             dma((2,)),
             dma((2,)),
             dma((len(STREAMS), 4)),
             dma((len(STREAMS), 4)),
-            dma((2,)),
-            dma((2,)),
+            dma((2, 2)),
+            dma((2, 2)),
             pltpu.SemaphoreType.REGULAR,
+            dma((7,)),
         ],
         compiler_params=pltpu.CompilerParams(
             has_side_effects=True, collective_id=0, vmem_limit_bytes=58 * 1024 * 1024

time: 104 us -> 102 us (0.981)
  the two profiles are of different devices: /device:TPU:4 before, /device:TPU:2 now
where the time goes in v4:
time: 102 us; the launch traced here: 101 us
  Pallas kernels  99.5 us (98%)
  local copies, waits for them, and re-layouts  1.88 us (2%)
    pallas_call x1, Pallas kernels, on_device(): pl.pallas_call(kernel, out_shape=jax.ShapeDtypeStruct((cells, width), bf1...  99.5 us

profile of v4, /device:TPU:2, one launch (start us, length us, event | category | flops | bytes accessed | tf_op | source)
XLA Modules:
  0.0 101.4 jit_solution(3023143603874714325)
XLA Ops:
  0.0 99.5 %shard_map.136 = bf16[128,2048]{1,0:T(8,128)(2,1)} custom-call(f32[2,8,8]{2,1,0:T(8,128)} %offset_ref.1, f32[8,33]{1,0:T(8,128)} %table_ref.1, f32[3,8]{1,0:T(4,128)} %bitcast.25, bf16[768,2048]{1,0:T(8,128)(2,1)} %bitcast.13, s32[1,768]{1,0:T(1,128)} %bitcast.21, s32[1,768]{1,0:T(1,128)} %bitcast.22, s32[1,768]{1,0:T(1,128)} %bitcast.23, ...), custom_call_target="tpu_custom_call" | custom-call | tf_op jit(solution)/shard_map/pallas_call | solution.py:428
  99.5 1.9 %copy.16 = bf16[1,128,2048]{2,1,0:T(8,128)(2,1)} copy(bf16[1,128,2048]{2,1,0:T(8,128)(2,1)} %bitcast.14) | data formatting | bytes 1048576

commit v5 on v4

--- a/solution.py
+++ b/solution.py
@@ -207,7 +207,7 @@
                     device_id_type=MESH,
                 ).start()
 
-        if first_band == 0:
+        if first_band == 2:
             for plan in range(2):
                 to_peer = (lax.broadcasted_iota(i32, (PEERS, blocks), 0) == numbers[plan]).astype(f32).astype(bf16)
                 lane_slot = lax.broadcasted_iota(i32, (128, blocks), 0) & (SLOTS - 1)

time: 102 us -> 109 us (1.069)
  Pallas kernels: 99.5 us -> 107 us
    pallas_call x1, Pallas kernels: 99.5 us -> 107 us  [on_device(): pl.pallas_call(kernel, out_shape=jax.ShapeDtypeStruct((cells, width), bf1...]
where the time goes in v5:
time: 109 us
  Pallas kernels  107 us (98%)
  local copies, waits for them, and re-layouts  1.88 us (2%)
    pallas_call x1, Pallas kernels, on_device(): pl.pallas_call(kernel, out_shape=jax.ShapeDtypeStruct((cells, width), bf1...  107 us

profile of v5, /device:TPU:2, one launch (start us, length us, event | category | flops | bytes accessed | tf_op | source)
XLA Modules:
  0.0 108.8 jit_solution(2245983422177273516)
XLA Ops:
  0.0 106.9 %shard_map.136 = bf16[128,2048]{1,0:T(8,128)(2,1)} custom-call(f32[2,8,8]{2,1,0:T(8,128)} %offset_ref.1, f32[8,33]{1,0:T(8,128)} %table_ref.1, f32[3,8]{1,0:T(4,128)} %bitcast.25, bf16[768,2048]{1,0:T(8,128)(2,1)} %bitcast.13, s32[1,768]{1,0:T(1,128)} %bitcast.21, s32[1,768]{1,0:T(1,128)} %bitcast.22, s32[1,768]{1,0:T(1,128)} %bitcast.23, ...), custom_call_target="tpu_custom_call" | custom-call | tf_op jit(solution)/shard_map/pallas_call | solution.py:428
  106.9 1.9 %copy.16 = bf16[1,128,2048]{2,1,0:T(8,128)(2,1)} copy(bf16[1,128,2048]{2,1,0:T(8,128)(2,1)} %bitcast.14) | data formatting | bytes 1048576
